TPU v7x, 256 devices: a whole 4x4x8 slice. The times are simulated.
256 devices in a mesh: dom: 64 (over z, y, core), grp: 4 (over x).
Axes of the slice: x: 4, y: 4, z: 8, core: 2. Of those that a mesh axis runs over, the one named last changes fastest.
Arguments:
- features: bfloat16 [4, 65536, 512], P('grp', 'dom'), may hold values from -6 to 6
- history: bfloat16 [2, 4, 65536, 512], P(None, 'grp', 'dom'), may hold values from -6 to 6
- adj_tiles: bfloat16 [4, 512, 4, 128, 128], P('grp', 'dom'), may hold values from -0.25 to 0.25
- blocks: int32 [4, 512, 4], P('grp', 'dom'), may hold values from 0 to 11, as said below
- send_list: int32 [4, 64, 64, 8], P('grp', 'dom'), may hold values from 0 to 1023
- counts: int32 [4, 64, 64], P('grp', 'dom'), may hold values from 0 to 8, as said below
- weights: bfloat16 [3, 512, 512], replicated, may hold values from -0.25 to 0.25
- cotangent: bfloat16 [4, 65536, 512], P('grp', 'dom'), may hold values from -16 to 16
Outputs:
- embedding: bfloat16 [4, 65536, 512], P('grp', 'dom')
- fresh_halo: bfloat16 [2, 4, 32768, 512], P(None, 'grp', 'dom')
- weight_grads: float32 [3, 512, 512], P(None, 'dom')
Inputs may be any that keep to these rules, and one draw needn't show every extreme that they name: `send_list`: entries at or past counts are not read. counts[g, q, p] is zero where q equals p; some owner uses all 8 slots for every other partition, and some partition gets 8 rows from every other owner. Entry 0 of the list of a partition's block b is b itself; entries 2 and 3 name halo blocks, at least 8.
All inputs are finite; a program needn't handle non-finite values.
Results may differ from a plain program's by a relative error of at most 0.012.
Values may be sent and summed in bfloat16 or wider, within the bound.
A program may use at most 128 MiB of HBM per device.

v0:
```python
import math

import jax
import jax.numpy as jnp
from jax import lax
from jax.sharding import PartitionSpec as P


def silu_slope(values):
    sigmoid_part = jax.nn.sigmoid(values)
    return sigmoid_part * (1.0 + values * (1.0 - sigmoid_part))


def pack_rows(source_rows, send_rows, live_counts):
    peer_count = send_rows.shape[0]
    capacity = send_rows.shape[1]
    picked = jnp.take(source_rows, send_rows.reshape(-1), axis=0)
    picked = picked.reshape(peer_count, capacity, source_rows.shape[1])
    in_use = jnp.arange(capacity, dtype=jnp.int32)[None, :] < live_counts[:, None]
    return jnp.where(in_use[:, :, None], picked, jnp.zeros((), jnp.bfloat16))


def aggregate(local_rows, halo_rows, tile_set, block_set):
    block_rows = tile_set.shape[-1]
    row_width = local_rows.shape[1]
    source = jnp.concatenate([local_rows, halo_rows], axis=0).reshape(-1, block_rows, row_width)
    picked = jnp.take(source, block_set.reshape(-1), axis=0)
    picked = picked.reshape(block_set.shape + (block_rows, row_width))
    mixed = jnp.einsum("bkij,bkjd->bid", tile_set, picked, preferred_element_type=jnp.float32)
    return mixed.reshape(-1, row_width)


def spread_back(grad_rows, tile_set, block_set):
    block_rows = tile_set.shape[-1]
    row_width = grad_rows.shape[1]
    local_blocks = grad_rows.shape[0] // block_rows
    by_block = grad_rows.reshape(-1, block_rows, row_width)
    contrib_terms = jnp.einsum(
        "bkij,bid->bkjd", tile_set, by_block, preferred_element_type=jnp.float32
    )
    owners = (
        block_set.reshape(1, -1) == jnp.arange(local_blocks, dtype=jnp.int32)[:, None]
    ).astype(jnp.float32)
    summed = jnp.dot(
        owners,
        contrib_terms.reshape(owners.shape[1], -1),
        precision=lax.Precision.HIGHEST,
        preferred_element_type=jnp.float32,
    )
    return summed.reshape(-1, row_width)


def body(features, history, adj_tiles, blocks, send_list, counts, weights, cotangent):
    node_rows = features[0]
    tile_set = adj_tiles[0]
    block_set = blocks[0]
    send_rows = send_list[0, 0]
    live_counts = counts[0, 0]
    row_width = node_rows.shape[1]
    pulled = (
        lax.all_to_all(
            pack_rows(node_rows, send_rows, live_counts),
            "dom",
            split_axis=0,
            concat_axis=0,
            tiled=True,
        ),
        lax.all_to_all(
            pack_rows(history[0, 0], send_rows, live_counts),
            "dom",
            split_axis=0,
            concat_axis=0,
            tiled=True,
        ),
        lax.all_to_all(
            pack_rows(history[1, 0], send_rows, live_counts),
            "dom",
            split_axis=0,
            concat_axis=0,
            tiled=True,
        ),
    )
    halo_inputs = [piece.reshape(-1, row_width) for piece in pulled]
    current = node_rows
    aggregated = []
    linear_out = []
    hidden_rows = []
    fresh_parts = []
    for layer_index in range(3):
        mixed = aggregate(current, halo_inputs[layer_index], tile_set, block_set).astype(
            jnp.bfloat16
        )
        product = jnp.dot(mixed, weights[layer_index], preferred_element_type=jnp.float32)
        aggregated.append(mixed)
        linear_out.append(product)
        if layer_index < 2:
            current = jax.nn.silu(product).astype(jnp.bfloat16)
            hidden_rows.append(current)
    node_out = linear_out[2].astype(jnp.bfloat16)
    fresh_parts = list(
        (
            lax.all_to_all(
                pack_rows(hidden_rows[0], send_rows, live_counts),
                "dom",
                split_axis=0,
                concat_axis=0,
                tiled=True,
            ),
            lax.all_to_all(
                pack_rows(hidden_rows[1], send_rows, live_counts),
                "dom",
                split_axis=0,
                concat_axis=0,
                tiled=True,
            ),
        )
    )
    fresh_halo = jnp.stack([piece.reshape(-1, row_width) for piece in fresh_parts])
    upstream = cotangent[0]
    partial_sums = [None, None, None]
    for layer_index in (2, 1, 0):
        partial_sums[layer_index] = lax.dot_general(
            aggregated[layer_index],
            upstream,
            (((0,), (0,)), ((), ())),
            preferred_element_type=jnp.float32,
        )
        if layer_index > 0:
            slope_in = lax.dot_general(
                upstream,
                weights[layer_index],
                (((1,), (1,)), ((), ())),
                preferred_element_type=jnp.float32,
            ).astype(jnp.bfloat16)
            back_rows = spread_back(slope_in, tile_set, block_set)
            upstream = (back_rows * silu_slope(linear_out[layer_index - 1])).astype(jnp.bfloat16)
    total_rows = lax.axis_size("grp") * lax.axis_size("dom") * node_rows.shape[0]
    stacked = jnp.stack(partial_sums) * (1.0 / math.sqrt(total_rows))
    replica_total = lax.psum(stacked.astype(jnp.bfloat16), "grp").astype(jnp.float32)
    weight_grads = lax.psum_scatter(replica_total, "dom", scatter_dimension=1, tiled=True)
    return (node_out[None], fresh_halo[:, None], weight_grads)


def solution(mesh):
    placed = (
        P("grp", "dom", None),
        P(None, "grp", "dom", None),
        P("grp", "dom", None, None, None),
        P("grp", "dom", None),
        P("grp", "dom", None, None),
        P("grp", "dom", None),
        P(),
        P("grp", "dom", None),
    )
    return jax.shard_map(
        body,
        mesh=mesh,
        in_specs=placed,
        out_specs=(P("grp", "dom", None), P(None, "grp", "dom", None), P(None, "dom", None)),
        check_vma=False,
    )
```

profile of v0, /device:TPU:2, one launch (start us, length us, event | category | flops | bytes accessed | tf_op | source)
XLA Modules:
  0.0 374.4 jit_solution(13997142385125871676)
XLA Ops:
  8.9 3.3 gather_fusion
  12.3 1.0 bitcast_select_fusion.4
  13.3 12.4 %all-to-all-start = ((bf16[64,8,512]{2,1,0:T(8,128)(2,1)}), bf16[64,8,512]{2,1,0:T(8,128)(2,1)}, u32[]{:S(2)}, u32[]{:S(2)}) async-start(bf16[64,8,512]{2,1,0:T(8,128)(2,1)} %bitcast_select_fusion.4), calls=%async_computation | async-start | bytes 1048576 | tf_op jit(solution)/shard_map/all_to_all | solution.py:61
  25.8 1.7 slice_bitcast_fusion.1
  27.5 2.6 gather_fusion.2
  30.1 2.6 gather_fusion.4
  32.8 10.3 %all-to-all-done = bf16[64,8,512]{2,1,0:T(8,128)(2,1)} async-done(((bf16[64,8,512]{2,1,0:T(8,128)(2,1)}), bf16[64,8,512]{2,1,0:T(8,128)(2,1)}, u32[]{:S(2)}, u32[]{:S(2)}) %all-to-all-start) | async-done | bytes 524320 | tf_op jit(solution)/shard_map/all_to_all | solution.py:61
  43.1 2.3 pad_maximum_fusion
  45.4 4.2 %gather_fusion.1 = bf16[32,128,512]{2,1,0:T(8,128)(2,1)} fusion(bf16[12,128,512]{2,1,0:T(8,128)(2,1)} %bitcast.138, s32[1024]{0:T(1024)S(1)} %pad_clamp_fusion), kind=kCustom, calls=%fused_computation.1.clone | custom fusion | bytes 8388736 | tf_op jit(solution)/shard_map/jit(_take)/gather | solution.py:27
  49.6 2.6 broadcast_select_fusion
  53.0 3.7 multiply_convert_fusion.3
  56.7 2.6 gather_fusion.6
  59.3 2.5 bitcast_select_fusion.1
  61.8 5.9 %all-to-all-start.1 = ((bf16[64,8,512]{2,1,0:T(8,128)(2,1)}), bf16[64,8,512]{2,1,0:T(8,128)(2,1)S(1)}, u32[]{:S(2)}, u32[]{:S(2)}) async-start(bf16[64,8,512]{2,1,0:T(8,128)(2,1)} %get-tuple-element.10), calls=%async_computation.1 | async-start | bytes 1048576 | tf_op jit(solution)/shard_map/all_to_all | solution.py:68
  67.7 2.1 convolution_convert_fusion.1
  69.8 4.5 %convolution_bitcast_fusion.1 = f32[8,4,128,512]{2,3,1,0:T(8,128)} fusion(bf16[8,128,512,1]{2,1,3,0:T(8,128)(2,1)S(1)} %bitcast.150, bf16[1,8,4,128,128]{4,3,2,1,0:T(8,128)(2,1)S(1)} %copy-done), kind=kOutput, calls=%fused_computation.12 | convolution fusion | flops 536870912 | bytes 10485760 | tf_op jit(solution)/shard_map/bkij,bid->bkjd/dot_general | solution.py:38
  74.3 10.4 %copy.29 = f32[4,8,128,512]{3,1,2,0:T(8,128)} copy(f32[4,8,128,512]{2,3,1,0:T(8,128)} %bitcast.127) | data formatting | bytes 16777216
  84.7 7.5 %fusion.22 = f32[8,65536]{1,0:T(8,128)} fusion(f32[32,65536]{1,0:T(8,128)} %bitcast.130, s32[32]{0:T(128)S(1)} %reshape_squeeze.5), kind=kOutput, calls=%fused_computation.67 | convolution fusion | flops 201326848 | bytes 10485888 | tf_op jit(solution)/shard_map/dot_general | solution.py:44
  92.2 3.3 reshape.126
  95.5 10.1 %all-to-all-start.2 = ((bf16[64,8,512]{2,1,0:T(8,128)(2,1)}), bf16[64,8,512]{2,1,0:T(8,128)(2,1)S(1)}, u32[]{:S(2)}, u32[]{:S(2)}) async-start(bf16[64,8,512]{2,1,0:T(8,128)(2,1)} %get-tuple-element.11), calls=%async_computation.2 | async-start | bytes 1048576 | tf_op jit(solution)/shard_map/all_to_all | solution.py:75
  105.9 1.3 pad_maximum_fusion.1
  107.2 4.2 %gather_fusion.3 = bf16[32,128,512]{2,1,0:T(8,128)(2,1)} fusion(bf16[12,128,512]{2,1,0:T(8,128)(2,1)} %bitcast.136, s32[1024]{0:T(1024)S(1)} %pad_clamp_fusion), kind=kCustom, calls=%fused_computation.6.clone | custom fusion | bytes 8388736 | tf_op jit(solution)/shard_map/jit(_take)/gather | solution.py:27
  111.4 2.6 broadcast_select_fusion.1
  116.1 1.4 multiply_convert_fusion.1
  117.5 1.7 convolution_bitcast_fusion.3
  119.2 1.8 convolution_convert_fusion
  121.0 2.3 all-to-all-done.2
  123.3 1.3 pad_maximum_fusion.2
  124.6 4.2 %gather_fusion.5 = bf16[32,128,512]{2,1,0:T(8,128)(2,1)} fusion(bf16[12,128,512]{2,1,0:T(8,128)(2,1)} %bitcast.137, s32[1024]{0:T(1024)S(1)} %pad_clamp_fusion), kind=kCustom, calls=%fused_computation.7.clone | custom fusion | bytes 8388736 | tf_op jit(solution)/shard_map/jit(_take)/gather | solution.py:27
  128.7 2.6 broadcast_select_fusion.2
  132.6 1.7 convolution_bitcast_fusion.2
  134.3 4.5 %convolution_bitcast_fusion = f32[8,4,128,512]{2,3,1,0:T(8,128)} fusion(bf16[8,128,512,1]{2,1,3,0:T(8,128)(2,1)S(1)} %bitcast.149, bf16[1,8,4,128,128]{4,3,2,1,0:T(8,128)(2,1)S(1)} %copy-done), kind=kOutput, calls=%fused_computation.11 | convolution fusion | flops 536870912 | bytes 10485760 | tf_op jit(solution)/shard_map/bkij,bid->bkjd/dot_general | solution.py:38
  138.9 10.4 %copy.30 = f32[4,8,128,512]{3,1,2,0:T(8,128)} copy(f32[4,8,128,512]{2,3,1,0:T(8,128)} %bitcast.128) | data formatting | bytes 16777216
  149.2 7.5 %fusion.21 = f32[8,65536]{1,0:T(8,128)} fusion(f32[32,65536]{1,0:T(8,128)} %bitcast.129, s32[32]{0:T(128)S(1)} %reshape_squeeze.5), kind=kOutput, calls=%fused_computation.66 | convolution fusion | flops 201326848 | bytes 10485888 | tf_op jit(solution)/shard_map/dot_general | solution.py:44
  156.8 3.4 reshape.129
  160.2 3.5 convolution_bitcast_fusion.4
  163.7 1.6 fusion
  165.4 53.3 %all-reduce.2.cloned.1.call-done = bf16[3,512,512]{2,1,0:T(8,128)(2,1)} async-done(((bf16[3,512,512]{2,1,0:T(8,128)(2,1)}), bf16[3,512,512]{2,1,0:T(8,128)(2,1)}) %all-reduce.2.cloned.1.call-update) | async-done | bytes 1572880 | tf_op jit(solution)/shard_map/psum | solution.py:139
  218.7 3.5 convert_element_type.78
  222.2 10.7 %all-to-all-start.3 = ((bf16[64,8,512]{2,1,0:T(8,128)(2,1)}), bf16[64,8,512]{2,1,0:T(8,128)(2,1)S(1)}, u32[]{:S(2)}, u32[]{:S(2)}) async-start(bf16[64,8,512]{2,1,0:T(8,128)(2,1)} %get-tuple-element.9), calls=%async_computation.3 | async-start | bytes 1048576 | tf_op jit(solution)/shard_map/all_to_all | solution.py:102
  232.9 2.0 gather_fusion.7
  234.9 1.0 bitcast_select_fusion
  235.9 14.6 %all-to-all-done.3 = bf16[64,8,512]{2,1,0:T(8,128)(2,1)S(1)} async-done(((bf16[64,8,512]{2,1,0:T(8,128)(2,1)}), bf16[64,8,512]{2,1,0:T(8,128)(2,1)S(1)}, u32[]{:S(2)}, u32[]{:S(2)}) %all-to-all-start.3) | async-done | bytes 524320 | tf_op jit(solution)/shard_map/all_to_all | solution.py:102
  250.6 5.8 %all-to-all-start.4 = ((bf16[64,8,512]{2,1,0:T(8,128)(2,1)}), bf16[64,8,512]{2,1,0:T(8,128)(2,1)S(1)}, u32[]{:S(2)}, u32[]{:S(2)}) async-start(bf16[64,8,512]{2,1,0:T(8,128)(2,1)} %bitcast_select_fusion), calls=%async_computation.4 | async-start | bytes 1048576 | tf_op jit(solution)/shard_map/all_to_all | solution.py:109
  256.3 3.1 fusion.1
  259.4 14.6 %all-to-all-done.4 = bf16[64,8,512]{2,1,0:T(8,128)(2,1)S(1)} async-done(((bf16[64,8,512]{2,1,0:T(8,128)(2,1)}), bf16[64,8,512]{2,1,0:T(8,128)(2,1)S(1)}, u32[]{:S(2)}, u32[]{:S(2)}) %all-to-all-start.4) | async-done | bytes 524320 | tf_op jit(solution)/shard_map/all_to_all | solution.py:109
  274.0 1.1 maximum_bitcast_fusion
  275.0 92.5 %reduce-scatter.2.cloned.1.call-done = f32[3,8,512]{2,1,0:T(8,128)} async-done(((f32[3,512,512]{2,1,0:T(8,128)}), f32[3,8,512]{2,1,0:T(8,128)}) %reduce-scatter.2.cloned.1.call-update) | async-done | bytes 49168 | tf_op jit(solution)/shard_map/reduce_scatter | solution.py:140
  (47 shorter events, 6.2 us)
Async XLA Ops:
  7.2 45.1 %copy-start = (bf16[1,8,4,128,128]{4,3,2,1,0:T(8,128)(2,1)S(1)}, bf16[1,8,4,128,128]{4,3,2,1,0:T(8,128)(2,1)}, u32[]{:S(2)}) copy-start(bf16[1,8,4,128,128]{4,3,2,1,0:T(8,128)(2,1)} %param.14) | copy-start | bytes 3145732
  12.3 13.4 %copy-start.11 = (s32[1,8,4]{1,2,0:T(4,128)S(1)}, s32[1,8,4]{1,2,0:T(4,128)}, u32[]{:S(2)}) copy-start(s32[1,8,4]{1,2,0:T(4,128)} %param.15) | copy-start | bytes 388
  13.3 29.8 %all-to-all-start = ((bf16[64,8,512]{2,1,0:T(8,128)(2,1)}), bf16[64,8,512]{2,1,0:T(8,128)(2,1)}, u32[]{:S(2)}, u32[]{:S(2)}) async-start(bf16[64,8,512]{2,1,0:T(8,128)(2,1)} %bitcast_select_fusion.4), calls=%async_computation | async-start | bytes 1048576 | tf_op jit(solution)/shard_map/all_to_all | solution.py:61
  30.1 13.0 %copy-start.1 = (bf16[1,1024,512]{2,1,0:T(8,128)(2,1)S(1)}, bf16[1,1024,512]{2,1,0:T(8,128)(2,1)}, u32[]{:S(2)}) copy-start(bf16[1,1024,512]{2,1,0:T(8,128)(2,1)} %param.12) | copy-start | bytes 3145732
  53.0 3.7 copy-start.5
  56.7 2.6 copy-start.3
  56.7 2.6 copy-start.4
  61.8 33.8 %all-to-all-start.1 = ((bf16[64,8,512]{2,1,0:T(8,128)(2,1)}), bf16[64,8,512]{2,1,0:T(8,128)(2,1)S(1)}, u32[]{:S(2)}, u32[]{:S(2)}) async-start(bf16[64,8,512]{2,1,0:T(8,128)(2,1)} %get-tuple-element.10), calls=%async_computation.1 | async-start | bytes 1048576 | tf_op jit(solution)/shard_map/all_to_all | solution.py:68
  95.5 27.8 %all-to-all-start.2 = ((bf16[64,8,512]{2,1,0:T(8,128)(2,1)}), bf16[64,8,512]{2,1,0:T(8,128)(2,1)S(1)}, u32[]{:S(2)}, u32[]{:S(2)}) async-start(bf16[64,8,512]{2,1,0:T(8,128)(2,1)} %get-tuple-element.11), calls=%async_computation.2 | async-start | bytes 1048576 | tf_op jit(solution)/shard_map/all_to_all | solution.py:75
  105.7 113.0 %all-reduce.2.cloned.1.call-start = ((), (), s32[]{:S(2)}) async-start(), calls=%async_computation.6 | async-start | bytes 3145728 | tf_op jit(solution)/shard_map/psum | solution.py:139
  114.0 1.6 copy-start.2
  114.0 2.0 copy-start.12
  131.4 1.2 copy-start.13
  132.2 2.2 copy-start.7
  132.6 1.7 copy-start.8
  156.8 3.4 copy-start.6
  160.2 3.5 copy-start.9
  160.2 3.5 copy-start.10
  165.3 202.2 %reduce-scatter.2.cloned.1.call-start = ((), (), s32[]{:S(2)}) async-start(), calls=%async_computation.7 | async-start | bytes 3194880 | tf_op jit(solution)/shard_map/reduce_scatter | solution.py:140
  222.2 28.4 %all-to-all-start.3 = ((bf16[64,8,512]{2,1,0:T(8,128)(2,1)}), bf16[64,8,512]{2,1,0:T(8,128)(2,1)S(1)}, u32[]{:S(2)}, u32[]{:S(2)}) async-start(bf16[64,8,512]{2,1,0:T(8,128)(2,1)} %get-tuple-element.9), calls=%async_computation.3 | async-start | bytes 1048576 | tf_op jit(solution)/shard_map/all_to_all | solution.py:102
  250.6 23.4 %all-to-all-start.4 = ((bf16[64,8,512]{2,1,0:T(8,128)(2,1)}), bf16[64,8,512]{2,1,0:T(8,128)(2,1)S(1)}, u32[]{:S(2)}, u32[]{:S(2)}) async-start(bf16[64,8,512]{2,1,0:T(8,128)(2,1)} %bitcast_select_fusion), calls=%async_computation.4 | async-start | bytes 1048576 | tf_op jit(solution)/shard_map/all_to_all | solution.py:109
Sparse Core Ops, SparseCore 0:
  165.4 53.2 all-reduce.1
  223.4 144.1 reduce-scatter.1
where the time goes:
time: 376 us; the launch traced here: 374 us
  waiting for transfers between devices  188 us (50%)
  local copies, waits for them, and re-layouts  57.8 us (15%)
  starting transfers between devices  45.2 us (12%)
  matrix products  45.1 us (12%)
  other arithmetic  24.2 us (6%)
  between operations  14.3 us (4%)
    reduce_scatter x1, waiting for transfers between devices, body(): lax.psum_scatter(replica_total, 'dom', scatter_dimension=1, tiled=True)  92.5 us
    psum x1, waiting for transfers between devices, body(): lax.psum(stacked.astype(jnp.bfloat16), 'grp').astype(jnp.float32)  53.3 us
    unnamed x32, local copies, waits for them, and re-layouts  23.5 us
    dot_general x2, matrix products, spread_back(): jnp.dot(owners, contrib_terms.reshape(owners.shape[1], -1), precision=lax...  15 us
    all_to_all x1, waiting for transfers between devices, body(): lax.all_to_all(pack_rows(hidden_rows[0], send_rows, live_counts), 'dom',...  14.6 us
    all_to_all x1, waiting for transfers between devices, body(): lax.all_to_all(pack_rows(hidden_rows[1], send_rows, live_counts), 'dom',...  14.6 us
    gather x5, local copies, waits for them, and re-layouts, pack_rows(): picked = jnp.take(source_rows, send_rows.reshape(-1), axis=0)  13.2 us
    gather x3, local copies, waits for them, and re-layouts, aggregate(): picked = jnp.take(source, block_set.reshape(-1), axis=0)  12.5 us
  transfers between devices with their start and end apart: 7, of which 6 were waited for; matrix products, arithmetic and copies ran while one was open for 15% of the time, Pallas kernels for 0%

commit v1 on v0

v1 whole, which is shorter than its diff:
```python
import functools
import math

import jax
import jax.numpy as jnp
from jax import lax
from jax.experimental import pallas as pl
from jax.experimental.pallas import tpu as pltpu
from jax.sharding import PartitionSpec as P

MESH = pl.DeviceIdType.MESH
F32 = jnp.float32
BF16 = jnp.bfloat16
STEP = 256


def dot(lhs, rhs):
    return jnp.dot(lhs, rhs, preferred_element_type=F32)


def step_kernel(
    nd, ng, scale,
    feat, hist, tiles, blocks, idx, w, cot,
    emb, fresh, wg,
    onehot, adj, adjt, wt, pk, rc, halo, hid, slope, mt, back, dm, grad,
    xs, xr, ds, dr, es, er,
    send_sem, recv_sem, xsend_sem, xrecv_sem, dsend_sem, drecv_sem, esend_sem, erecv_sem,
):
    me = lax.axis_index("dom")
    mx = lax.axis_index("grp")
    rows, width = feat.shape
    slots = nd * 8
    blk = tiles.shape[2]
    local_blocks = rows // blk
    halo_blocks = slots // blk
    cols = width // ng

    barrier = pltpu.get_barrier_semaphore()

    def greet(j, carry):
        peer = lax.rem(me + j, nd)
        pl.semaphore_signal(barrier, inc=1, device_id={"dom": peer}, device_id_type=MESH)
        return carry

    lax.fori_loop(1, nd, greet, 0)
    for o in range(1, ng):
        pl.semaphore_signal(
            barrier, inc=1, device_id={"grp": lax.rem(mx + o, ng)}, device_id_type=MESH
        )

    def dom_copy(src, dst, ssem, rsem, peer):
        return pltpu.make_async_remote_copy(
            src_ref=src, dst_ref=dst, send_sem=ssem, recv_sem=rsem,
            device_id={"dom": peer}, device_id_type=MESH,
        )

    def grp_copy(src, dst, ssem, rsem, peer):
        return pltpu.make_async_remote_copy(
            src_ref=src, dst_ref=dst, send_sem=ssem, recv_sem=rsem,
            device_id={"grp": peer}, device_id_type=MESH,
        )

    def spread(src, dst, ssem, rsem):
        def pair(j, carry):
            up = lax.rem(me + j, nd)
            down = lax.rem(me + nd - j, nd)
            dom_copy(src.at[up], dst.at[me], ssem, rsem, up).start()
            dom_copy(src.at[down], dst.at[me], ssem, rsem, down).start()
            return carry

        lax.fori_loop(1, nd // 2, pair, 0)
        far = lax.rem(me + nd // 2, nd)
        dom_copy(src.at[far], dst.at[me], ssem, rsem, far).start()

    def spread_whole(src, dst, ssem, rsem):
        far = lax.rem(me + nd // 2, nd)
        return dom_copy(src.at[pl.ds(0, nd - 1)], dst.at[pl.ds(0, nd - 1)], ssem, rsem, far)

    def chunked(total, fn, size=STEP):
        def one(c, carry):
            fn(c, pl.multiple_of(c * size, size))
            return carry

        lax.fori_loop(0, total // size, one, 0)

    def make_onehot(c, at):
        column = lax.broadcasted_iota(jnp.int32, (STEP, rows), 1)
        hit = column == idx[pl.ds(at, STEP), :]
        onehot[pl.ds(at, STEP), :] = jnp.where(hit, 1.0, 0.0).astype(BF16)

    def pack(source, slot):
        def one(c, at):
            picked = dot(onehot[pl.ds(at, STEP), :], source[...])
            pk[slot, pl.ds(c * (STEP // 8), STEP // 8)] = picked.reshape(
                STEP // 8, 8, width
            ).astype(BF16)

        chunked(slots, one)

    chunked(slots, make_onehot)
    pack(feat, 0)
    for i in range(3):
        rc[i, me] = jnp.zeros((8, width), BF16)
    for i in range(2):
        fresh[i, me] = jnp.zeros((8, width), BF16)
    pl.semaphore_wait(barrier, nd - 1 + ng - 1)
    spread(pk.at[0], rc.at[0], send_sem.at[0], recv_sem.at[0])
    pack(hist.at[0], 1)
    spread(pk.at[1], rc.at[1], send_sem.at[1], recv_sem.at[1])
    pack(hist.at[1], 2)
    spread(pk.at[2], rc.at[2], send_sem.at[2], recv_sem.at[2])

    def build(b, carry):
        at = pl.multiple_of(b * blk, blk)
        t = [tiles[b, k].astype(F32) for k in range(4)]
        name = [blocks[b, k] for k in range(4)]

        def on(k, j):
            return jnp.where(name[k] == j, 1.0, 0.0).astype(F32)

        own_t = t[0].T
        pick_t = t[1].T
        for j in range(local_blocks):
            own = jnp.where(b == j, 1.0, 0.0).astype(F32)
            there = on(1, j)
            adj[pl.ds(at, blk), j * blk:(j + 1) * blk] = (own * t[0] + there * t[1]).astype(BF16)
            adjt[j * blk:(j + 1) * blk, pl.ds(at, blk)] = (own * own_t + there * pick_t).astype(BF16)
        for j in range(local_blocks, local_blocks + halo_blocks):
            mix = on(1, j) * t[1] + on(2, j) * t[2] + on(3, j) * t[3]
            adj[pl.ds(at, blk), j * blk:(j + 1) * blk] = mix.astype(BF16)
        return carry

    lax.fori_loop(0, local_blocks, build, 0)
    for l in (1, 2):
        for c in range(width // STEP):
            part = w[l, c * STEP:(c + 1) * STEP, :].astype(F32)
            wt[l - 1, :, c * STEP:(c + 1) * STEP] = part.T.astype(BF16)

    def pull_back(source, l):
        def first(c, at):
            dm[pl.ds(at, STEP), :] = dot(source[pl.ds(at, STEP), :], wt[l - 1]).astype(BF16)

        def second(c, at):
            back[pl.ds(at, STEP), :] = dot(adjt[pl.ds(at, STEP), :], dm[...])

        chunked(rows, first)
        chunked(rows, second)

    def layer(source, l):
        def flat(c, at):
            part = rc[l, pl.ds(c * (STEP // 8), STEP // 8)]
            halo[pl.ds(at, STEP), :] = part.astype(F32).reshape(STEP, width).astype(BF16)

        chunked(slots, flat)

        def one(c, at):
            mixed = dot(adj[pl.ds(at, STEP), :rows], source[...])
            mixed += dot(adj[pl.ds(at, STEP), rows:], halo[...])
            mixed = mixed.astype(BF16)
            mt[l, :, pl.ds(at, STEP)] = mixed.T
            z = dot(mixed, w[l])
            if l == 2:
                emb[pl.ds(at, STEP), :] = z.astype(BF16)
            else:
                s = 1.0 / (1.0 + jnp.exp(-z))
                hid[l, pl.ds(at, STEP), :] = (z * s).astype(BF16)
                slope[l, pl.ds(at, STEP), :] = s * (1.0 + z * (1.0 - s))

        chunked(rows, one)

    def gate(l):
        def one(c, at):
            grad[l, pl.ds(at, STEP), :] = (
                back[pl.ds(at, STEP), :] * slope[l, pl.ds(at, STEP), :]
            ).astype(BF16)

        chunked(rows, one)

    def weight_part(l, source):
        def one(c, at):
            part = dot(mt[l, pl.ds(at, STEP), :], source[...])
            for j in range(ng):
                xs[l, j, pl.ds(at, STEP), :] = part[:, j * cols:(j + 1) * cols].astype(BF16)

        chunked(width, one)
        for o in (1, 3, 2):
            peer = lax.rem(mx + o, ng)
            grp_copy(
                xs.at[l, peer], xr.at[l, mx], xsend_sem.at[l], xrecv_sem.at[l], peer
            ).start()

    def weight_whole(l):
        return grp_copy(
            xs.at[l, pl.ds(0, ng - 1)], xr.at[l, pl.ds(0, ng - 1)],
            xsend_sem.at[l], xrecv_sem.at[l], lax.rem(mx + 1, ng),
        )

    def weight_sum(l):
        weight_whole(l).wait_recv()

        def one(c, at):
            total = xs[l, mx, pl.ds(at, STEP), :].astype(F32)
            for o in range(1, ng):
                total += xr[l, lax.rem(mx + o, ng), pl.ds(at, STEP), :].astype(F32)
            ds[pl.ds(c * (STEP // 8), STEP // 8), l] = total.reshape(
                STEP // 8, 8, cols
            ).astype(BF16)

        chunked(width, one)

    pull_back(cot, 2)

    inputs = (feat, hid.at[0], hid.at[1])
    spread_whole(pk.at[0], rc.at[0], send_sem.at[0], recv_sem.at[0]).wait_recv()
    layer(inputs[0], 0)
    pack(hid.at[0], 3)
    spread(pk.at[3], fresh.at[0], send_sem.at[3], recv_sem.at[3])

    spread_whole(pk.at[1], rc.at[1], send_sem.at[1], recv_sem.at[1]).wait_recv()
    layer(inputs[1], 1)
    gate(1)
    weight_part(1, grad.at[1])
    pack(hid.at[1], 4)
    spread(pk.at[4], fresh.at[1], send_sem.at[4], recv_sem.at[4])
    pull_back(grad.at[1], 1)
    gate(0)
    weight_part(0, grad.at[0])

    spread_whole(pk.at[2], rc.at[2], send_sem.at[2], recv_sem.at[2]).wait_recv()
    layer(inputs[2], 2)
    weight_part(2, cot)

    for l in (1, 0, 2):
        weight_sum(l)
    dr[me] = ds[me]
    spread(ds, dr, dsend_sem, drecv_sem)
    spread_whole(ds, dr, dsend_sem, drecv_sem).wait_recv()
    es[...] = jnp.sum(dr[...].astype(F32), axis=0) * scale
    er[mx] = es[...]
    for o in (1, 3, 2):
        grp_copy(es, er.at[mx], esend_sem, erecv_sem, lax.rem(mx + o, ng)).start()
    whole = grp_copy(
        er.at[pl.ds(0, ng - 1)], er.at[pl.ds(0, ng - 1)], esend_sem, erecv_sem, lax.rem(mx + 1, ng)
    )
    whole.wait_recv()
    for j in range(ng):
        wg[:, :, j * cols:(j + 1) * cols] = er[j]

    for i in range(2):
        spread_whole(pk.at[3 + i], fresh.at[i], send_sem.at[3 + i], recv_sem.at[3 + i]).wait_recv()
    for i in range(5):
        target = rc.at[i] if i < 3 else fresh.at[i - 3]
        spread_whole(pk.at[i], target, send_sem.at[i], recv_sem.at[i]).wait_send()
    for l in range(3):
        weight_whole(l).wait_send()
    spread_whole(ds, dr, dsend_sem, drecv_sem).wait_send()
    whole.wait_send()


def body(nd, ng, features, history, adj_tiles, blocks, send_list, counts, weights, cotangent):
    rows, width = features.shape[1], features.shape[2]
    slots = nd * 8
    cols = width // ng
    in_use = jnp.arange(8, dtype=jnp.int32)[None, :] < counts[0, 0][:, None]
    idx = jnp.where(in_use, send_list[0, 0], -1).reshape(slots, 1)
    scale = 1.0 / math.sqrt(ng * nd * rows)
    vmem = pl.BlockSpec(memory_space=pltpu.VMEM)
    smem = pl.BlockSpec(memory_space=pltpu.SMEM)
    dma = pltpu.SemaphoreType.DMA
    emb, fresh, wg = pl.pallas_call(
        functools.partial(step_kernel, nd, ng, scale),
        out_shape=(
            jax.ShapeDtypeStruct((rows, width), BF16),
            jax.ShapeDtypeStruct((2, nd, 8, width), BF16),
            jax.ShapeDtypeStruct((3, 8, width), F32),
        ),
        in_specs=[vmem, vmem, vmem, smem, vmem, vmem, vmem],
        out_specs=(vmem, vmem, vmem),
        scratch_shapes=[
            pltpu.VMEM((slots, rows), BF16),
            pltpu.VMEM((rows, rows + slots), BF16),
            pltpu.VMEM((rows, rows), BF16),
            pltpu.VMEM((2, width, width), BF16),
            pltpu.VMEM((5, nd, 8, width), BF16),
            pltpu.VMEM((3, nd, 8, width), BF16),
            pltpu.VMEM((slots, width), BF16),
            pltpu.VMEM((2, rows, width), BF16),
            pltpu.VMEM((2, rows, width), F32),
            pltpu.VMEM((3, width, rows), BF16),
            pltpu.VMEM((rows, width), F32),
            pltpu.VMEM((rows, width), BF16),
            pltpu.VMEM((2, rows, width), BF16),
            pltpu.VMEM((3, ng, width, cols), BF16),
            pltpu.VMEM((3, ng, width, cols), BF16),
            pltpu.VMEM((nd, 3, 8, cols), BF16),
            pltpu.VMEM((nd, 3, 8, cols), BF16),
            pltpu.VMEM((3, 8, cols), F32),
            pltpu.VMEM((ng, 3, 8, cols), F32),
            dma((5,)), dma((5,)), dma((3,)), dma((3,)), dma, dma, dma, dma,
        ],
        compiler_params=pltpu.CompilerParams(
            collective_id=0, has_side_effects=True, vmem_limit_bytes=62 * 1024 * 1024
        ),
        name="gnn_step",
    )(
        features[0], history[:, 0], adj_tiles[0], blocks[0], idx, weights, cotangent[0]
    )
    return emb[None], fresh.reshape(2, 1, slots, width), wg


def solution(mesh):
    nd, ng = mesh.shape["dom"], mesh.shape["grp"]
    placed = (
        P("grp", "dom", None),
        P(None, "grp", "dom", None),
        P("grp", "dom", None, None, None),
        P("grp", "dom", None),
        P("grp", "dom", None, None),
        P("grp", "dom", None),
        P(),
        P("grp", "dom", None),
    )
    return jax.shard_map(
        functools.partial(body, nd, ng),
        mesh=mesh,
        in_specs=placed,
        out_specs=(P("grp", "dom", None), P(None, "grp", "dom", None), P(None, "dom", None)),
        check_vma=False,
    )
```

time: 376 us -> 95 us (0.25)
  waiting for transfers between devices: 188 us -> 0 us
  Pallas kernels: 0 us -> 85.2 us
  local copies, waits for them, and re-layouts: 57.8 us -> 6.34 us
  starting transfers between devices: 45.2 us -> 0 us
  matrix products: 45.1 us -> 0 us
  other arithmetic: 24.2 us -> 1.46 us
  between operations: 14.3 us -> 0.68 us
    reduce_scatter x1 -> x0, waiting for transfers between devices: 92.5 us -> none  [body(): lax.psum_scatter(replica_total, 'dom', scatter_dimension=1, tiled=True)]
    pallas_call x0 -> x1, Pallas kernels: none -> 85.2 us  [body(): pl.pallas_call(functools.partial(step_kernel, nd, ng, scale), out_shape=(...]
    psum x1 -> x0, waiting for transfers between devices: 53.3 us -> none  [body(): lax.psum(stacked.astype(jnp.bfloat16), 'grp').astype(jnp.float32)]
    dot_general x15 -> x0, matrix products: 45.1 us -> none  [the longest x2 15 us: spread_back(): jnp.dot(owners, contrib_terms.reshape(owners.shape[1], -1), precision=lax...]
    all_to_all x5 -> x0, starting transfers between devices: 44.9 us -> none  [the longest x1 12.4 us: body(): lax.all_to_all(pack_rows(node_rows, send_rows, live_counts), 'dom', split...]
    all_to_all x5 -> x0, waiting for transfers between devices: 41.9 us -> none  [the longest x1 14.6 us: body(): lax.all_to_all(pack_rows(hidden_rows[0], send_rows, live_counts), 'dom',...]
    gather x8 -> x0, local copies, waits for them, and re-layouts: 25.7 us -> none  [the longest x5 13.2 us: pack_rows(): picked = jnp.take(source_rows, send_rows.reshape(-1), axis=0)]
    unnamed x32 -> x8, local copies, waits for them, and re-layouts: 23.5 us -> 4.72 us
  transfers between devices with their start and end apart: 7 -> 0, of which waited for: 6 -> 0; matrix products, arithmetic and copies ran while one was open for 15% -> 0% of each run, Pallas kernels for 0% -> 0%
where the time goes in v1:
time: 95 us; the launch traced here: 93.7 us
  Pallas kernels  85.2 us (90%)
  local copies, waits for them, and re-layouts  6.34 us (7%)
  other arithmetic  1.46 us (2%)
    pallas_call x1, Pallas kernels, body(): pl.pallas_call(functools.partial(step_kernel, nd, ng, scale), out_shape=(...  85.2 us
    unnamed x8, local copies, waits for them, and re-layouts  4.72 us

profile of v1, /device:TPU:2, one launch (start us, length us, event | category | flops | bytes accessed | tf_op | source)
XLA Modules:
  0.0 93.7 jit_solution(14706481923644892970)
XLA Ops:
  0.6 1.3 %copy.17.blocks = s32[8,4]{1,0:T(8,128)} copy(s32[8,4]{0,1:T(4,128)} %bitcast.18) | data formatting | bytes 256 | tf_op jit(solution)/shard_map/squeeze | solution.py:306
  2.0 0.7 iota_compare_fusion
  2.7 0.8 copy.14
  3.5 0.1 lt.30
  3.6 0.1 squeeze.24
  3.8 0.7 broadcast_select_fusion.idx
  4.5 85.2 %gnn_step.1 = (bf16[1024,512]{1,0:T(8,128)(2,1)}, bf16[2,64,8,512]{3,2,1,0:T(8,128)(2,1)}, f32[3,8,512]{2,1,0:T(8,128)}) custom-call(bf16[1024,512]{1,0:T(8,128)(2,1)} %bitcast.15, bf16[2,1024,512]{2,1,0:T(8,128)(2,1)} %bitcast.12, bf16[8,4,128,128]{3,2,1,0:T(8,128)(2,1)} %bitcast.16, s32[8,4]{1,0:T(8,128)} %copy.17.blocks, ...), custom_call_target="tpu_custom_call" | custom-call | tf_op jit(solution)/shard_map/gnn_step/pallas_call | solution.py:270
  89.7 0.0 copy-start
  89.7 0.0 copy-start.1
  89.8 2.3 %copy.22 = bf16[1,1024,512]{2,1,0:T(8,128)(2,1)} copy(bf16[1,1024,512]{2,1,0:T(8,128)(2,1)} %bitcast.14) | data formatting | bytes 2097152
  92.1 0.0 copy-done
  92.1 1.0 %copy.23 = bf16[2,1,512,512]{3,2,1,0:T(8,128)(2,1)} copy(bf16[2,1,512,512]{3,2,1,0:T(8,128)(2,1)S(1)} %bitcast.13) | data formatting | bytes 2097152
  93.1 0.0 copy-done.1
  93.1 0.6 copy.24
Async XLA Ops:
  89.7 2.4 %copy-start = (bf16[2,64,8,512]{3,2,1,0:T(8,128)(2,1)S(1)}, bf16[2,64,8,512]{3,2,1,0:T(8,128)(2,1)}, u32[]{:S(2)}) copy-start(bf16[2,64,8,512]{3,2,1,0:T(8,128)(2,1)} %get-tuple-element.7) | copy-start | bytes 3145732
  89.7 3.3 %copy-start.1 = (f32[3,8,512]{2,1,0:T(8,128)S(1)}, f32[3,8,512]{2,1,0:T(8,128)}, u32[]{:S(2)}) copy-start(f32[3,8,512]{2,1,0:T(8,128)} %get-tuple-element.20) | copy-start | bytes 147460
